TPU v7x, 512 devices: a whole 4x4x16 slice. The times are simulated.
512 devices in a mesh: dp: 8 (over z_hi, core), expert: 64 (over y, x, z_lo).
Axes of the slice: x: 4, y: 4, z: 16 (z_hi: 4, z_lo: 4; z = z_hi * 4 + z_lo), core: 2. Of those that a mesh axis runs over, the one named last changes fastest.
Arguments:
- tokens: bfloat16 [8192, 3584], P('expert', 'dp'), may hold values from -6 to 6
- out_grad: bfloat16 [8192, 3584], P('expert', 'dp'), may hold values from -6 to 6
- gate_up_weight: bfloat16 [64, 3584, 2048], P('expert', 'dp'), may hold values from -0.09375 to 0.09375
- down_weight: bfloat16 [64, 1024, 3584], P('expert', None, 'dp'), may hold values from -0.1875 to 0.1875
- routes: int32 [8192, 2], P('expert'), may hold values from 0 to 63, all different within a row; in each aligned block of 128 rows (0 to 127, 128 to 255, ...) at most 8 rows name the same one
- route_weight: float32 [8192, 2], P('expert'), may hold values from 0.1 to 1
- swapped: int32 [4], replicated, may hold values from 0 to 31, as said below
Outputs:
- layer_out: bfloat16 [8192, 3584], P('expert', 'dp')
- token_grad: bfloat16 [8192, 3584], P('expert', 'dp')
- down_grad: bfloat16 [64, 1024, 3584], P('expert', None, 'dp')
Inputs may be any that keep to these rules, and one draw needn't show every extreme that they name: `routes`: among the rows of each block of 128 consecutive tokens, no expert is named more than 8 times, a bound that some block reaches; a token names different experts. `swapped`: 4 different device numbers; device 0 and device 32 - 1 are always among them.
All inputs are finite; a program needn't handle non-finite values.
Results may differ from a plain program's by a relative error of at most 0.023.
Values may be sent and summed in bfloat16 or wider, within the bound.
A program may use at most 64 MiB of HBM per device.

v0:
```python
import jax
import jax.numpy as jnp
from jax import lax
from jax.sharding import PartitionSpec as P


def shifted(block, axis, distance):
    devices = range(lax.axis_size(axis))
    route = [((i - distance) % len(devices), i) for i in devices]
    return lax.ppermute(block, axis, route)


def gate_grads(gate_val, up_val, hidden_grad):
    sig = jax.nn.sigmoid(gate_val)
    act = gate_val * sig
    gate_grad = hidden_grad * up_val * sig * (1.0 + gate_val * (1.0 - sig))
    up_grad = hidden_grad * act
    return (gate_grad, up_grad)


def on_device(tokens, out_grad, gate_up_weight, down_weight, routes, route_weight, swapped):
    experts = lax.axis_size("expert")
    half = experts // 2
    token_count = tokens.shape[0]
    width_block = tokens.shape[1]
    top_count = routes.shape[1]
    hidden_width = down_weight.shape[1]
    capacity = max(2, 2 * token_count * top_count // experts)
    row_count = token_count * top_count
    buffer_rows = experts * capacity
    device_id = lax.axis_index("expert")
    moved = jnp.any(swapped[:, None] == jnp.arange(half, dtype=jnp.int32)[None, :], axis=0)
    self_moved = moved[device_id % half]
    flat = routes.reshape(-1)
    target = jnp.where(moved[flat % half], (flat + half) % experts, flat)
    onehot = (target[:, None] == jnp.arange(experts, dtype=jnp.int32)[None, :]).astype(jnp.int32)
    slot = jnp.sum(jnp.cumsum(onehot, axis=0) * onehot, axis=1) - 1
    spot = target * capacity + slot
    row_grad = (route_weight[:, :, None] * out_grad[:, None, :].astype(jnp.float32)).astype(
        jnp.bfloat16
    )
    row_grad = row_grad.reshape(row_count, width_block)
    token_rows = jnp.repeat(tokens, top_count, axis=0)
    send_tokens = jnp.zeros((buffer_rows, width_block), jnp.bfloat16).at[spot].set(token_rows)
    send_grads = jnp.zeros((buffer_rows, width_block), jnp.bfloat16).at[spot].set(row_grad)
    recv_tokens, recv_grads = (
        lax.all_to_all(
            send_tokens.reshape(experts, capacity, width_block),
            "expert",
            split_axis=0,
            concat_axis=0,
            tiled=True,
        ),
        lax.all_to_all(
            send_grads.reshape(experts, capacity, width_block),
            "expert",
            split_axis=0,
            concat_axis=0,
            tiled=True,
        ),
    )
    recv_tokens = recv_tokens.reshape(buffer_rows, width_block)
    recv_grads = recv_grads.reshape(buffer_rows, width_block)
    moved_gate_up, moved_down = shifted((gate_up_weight, down_weight), "expert", half)
    local_gate_up = jnp.where(self_moved, moved_gate_up, gate_up_weight)[0]
    local_down = jnp.where(self_moved, moved_down, down_weight)[0]
    gate_up_part = jnp.dot(recv_tokens, local_gate_up, preferred_element_type=jnp.float32)
    gate_up = lax.psum(gate_up_part.astype(jnp.bfloat16), "dp").astype(jnp.float32)
    gate_val = gate_up[:, :hidden_width]
    up_val = gate_up[:, hidden_width:]
    hidden = (jax.nn.silu(gate_val) * up_val).astype(jnp.bfloat16)
    row_out = jnp.dot(hidden, local_down, preferred_element_type=jnp.float32).astype(jnp.bfloat16)
    row_out = row_out.reshape(experts, capacity, width_block)
    back_out = lax.all_to_all(row_out, "expert", split_axis=0, concat_axis=0, tiled=True)
    hidden_part = lax.dot_general(
        recv_grads, local_down, (((1,), (1,)), ((), ())), preferred_element_type=jnp.float32
    )
    hidden_grad = lax.psum(hidden_part.astype(jnp.bfloat16), "dp").astype(jnp.float32)
    gate_grad, up_grad = gate_grads(gate_val, up_val, hidden_grad)
    gate_up_grad = jnp.concatenate([gate_grad, up_grad], axis=1).astype(jnp.bfloat16)
    row_dx = lax.dot_general(
        gate_up_grad, local_gate_up, (((1,), (1,)), ((), ())), preferred_element_type=jnp.float32
    ).astype(jnp.bfloat16)
    row_dx = row_dx.reshape(experts, capacity, width_block)
    expert_grad = lax.dot_general(
        hidden, recv_grads, (((0,), (0,)), ((), ())), preferred_element_type=jnp.float32
    ).astype(jnp.bfloat16)
    down_grad = expert_grad[None]
    back_dx = lax.all_to_all(row_dx, "expert", split_axis=0, concat_axis=0, tiled=True)
    out_rows = back_out.reshape(buffer_rows, width_block)[spot].reshape(
        token_count, top_count, width_block
    )
    dx_rows = back_dx.reshape(buffer_rows, width_block)[spot].reshape(
        token_count, top_count, width_block
    )
    layer_out = jnp.sum(route_weight[:, :, None] * out_rows.astype(jnp.float32), axis=1).astype(
        jnp.bfloat16
    )
    token_grad = jnp.sum(dx_rows.astype(jnp.float32), axis=1).astype(jnp.bfloat16)
    return (layer_out, token_grad, down_grad)


def solution(mesh):
    return jax.shard_map(
        on_device,
        mesh=mesh,
        in_specs=(
            P("expert", "dp"),
            P("expert", "dp"),
            P("expert", "dp", None),
            P("expert", None, "dp"),
            P("expert", None),
            P("expert", None),
            P(),
        ),
        out_specs=(P("expert", "dp"), P("expert", "dp"), P("expert", None, "dp")),
        check_vma=False,
    )
```

profile of v0, /device:TPU:1, one launch (start us, length us, event | category | flops | bytes accessed | tf_op | source)
XLA Modules:
  0.0 371.7 jit_solution(16007969242159612189)
XLA Ops:
  10.6 4.5 %select_reduce_fusion = (pred[256]{0:T(512)(128)(4,1)S(1)}, pred[256]{0:T(512)(128)(4,1)S(1)}, pred[256]{0:T(512)(128)(4,1)S(1)}, pred[256]{0:T(512)(128)(4,1)S(...) fusion(pred[]{:T(512)} %bitcast.25, ...), kind=kLoop, calls=%fused_computation.54 | loop fusion | flops 13056 | bytes 7687 | tf_op jit(solution)/shard_map/gather | solution.py:35
  15.1 15.6 %fusion.31 = (s32[256]{0:T(256)S(1)}, pred[256]{0:T(512)(128)(4,1)S(1)}) fusion(s32[256]{0:T(256)S(1)} %reshape.221, pred[256]{0:T(512)(128)(4,1)S(1)} %get-tuple-element.34, pred[256]{0:T(512)(128)(4,1)S(1)} %get-tuple-element.33, pred[256]{0:T(512)(128)(4,1)S(1)} %get-tuple-element.28, pred[256]{0:T(512)(128)(4,1)S(1)} %get-tuple-element.29, ...), kind=kLoop, calls=%fused_computation.93 | loop fusion | flops 9728 | bytes 8985 | tf_op jit(solution)/shard_map/jit(_where)/select_n | solution.py:35
  34.3 2.4 scatter_custom_fusion.1
  36.7 12.5 %all-to-all-start.2 = ((bf16[64,8,448]{2,1,0:T(8,128)(2,1)}), bf16[64,8,448]{2,1,0:T(8,128)(2,1)S(1)}, u32[]{:S(2)}, u32[]{:S(2)}) async-start(bf16[64,8,448]{2,1,0:T(8,128)(2,1)} %bitcast.43), calls=%async_computation.2 | async-start | bytes 1048576 | tf_op jit(solution)/shard_map/all_to_all | solution.py:54
  49.2 4.5 %collective-permute-start = (bf16[1,448,2048]{2,1,0:T(8,128)(2,1)}, bf16[1,448,2048]{2,1,0:T(8,128)(2,1)}, u32[]{:S(2)}, u32[]{:S(2)}) collective-permute-start(bf16[1,448,2048]{2,1,0:T(8,128)(2,1)} %param.9), channel_id=1, source_target_pairs={{32,0},{33,1},{34,2},{35,3},{36,4},{37,5},{38,6},{39,7},{40,8},{41... | collective-permute-start | bytes 5505032 | tf_op jit(solution)/shard_map/ppermute | solution.py:10
  54.3 2.3 scatter_custom_fusion
  56.6 10.3 %all-to-all-done.2 = bf16[64,8,448]{2,1,0:T(8,128)(2,1)S(1)} async-done(((bf16[64,8,448]{2,1,0:T(8,128)(2,1)}), bf16[64,8,448]{2,1,0:T(8,128)(2,1)S(1)}, u32[]{:S(2)}, u32[]{:S(2)}) %all-to-all-start.2) | async-done | bytes 458784 | tf_op jit(solution)/shard_map/all_to_all | solution.py:54
  66.8 4.9 %all-to-all-start = ((bf16[64,8,448]{2,1,0:T(8,128)(2,1)}), bf16[64,8,448]{2,1,0:T(8,128)(2,1)S(1)}, u32[]{:S(2)}, u32[]{:S(2)}) async-start(bf16[64,8,448]{2,1,0:T(8,128)(2,1)} %bitcast.36), calls=%async_computation | async-start | bytes 1048576 | tf_op jit(solution)/shard_map/all_to_all | solution.py:47
  71.8 4.8 %collective-permute-start.1 = (bf16[1,1024,448]{1,2,0:T(8,128)(2,1)}, bf16[1,1024,448]{1,2,0:T(8,128)(2,1)S(1)}, u32[]{:S(2)}, u32[]{:S(2)}) collective-permute-start(bf16[1,1024,448]{1,2,0:T(8,128)(2,1)} %param.10), channel_id=1, source_target_pairs={{32,0},{33,1},{34,2},{35,3},{36,4},{37,5},{38,6},{39,7},{40,8},{41... | collective-permute-start | bytes 2752520 | tf_op jit(solution)/shard_map/ppermute | solution.py:10
  76.7 47.6 %collective-permute-done.1 = bf16[1,1024,448]{1,2,0:T(8,128)(2,1)S(1)} collective-permute-done((bf16[1,1024,448]{1,2,0:T(8,128)(2,1)}, bf16[1,1024,448]{1,2,0:T(8,128)(2,1)S(1)}, u32[]{:S(2)}, u32[]{:S(2)}) %collective-permute-start.1) | collective-permute-done | bytes 917536 | tf_op jit(solution)/shard_map/ppermute | solution.py:10
  125.2 2.4 convolution_convert_fusion.1
  127.6 4.8 %convolution_convert_fusion = bf16[512,2048]{1,0:T(8,128)(2,1)} fusion(bf16[1,448,2048]{2,1,0:T(8,128)(2,1)} %collective-permute-done, bf16[1,448,2048]{2,1,0:T(8,128)(2,1)S(1)} %copy-done.2, pred[]{:T(512)} %bitcast.38, bf16[64,8,448]{2,1,0:T(8,128)(2,1)S(1)} %all-to-all-done), kind=kOutput, calls=%fused_computation.4 | convolution fusion | flops 941490176 | bytes 6225921 | tf_op jit(solution)/shard_map/dot_general | solution.py:67
  132.4 171.7 %all-reduce.3.cloned.1.call-done = (bf16[512,2048]{1,0:T(8,128)(2,1)}, bf16[512,1024]{1,0:T(8,128)(2,1)}) async-done(((bf16[512,2048]{1,0:T(8,128)(2,1)}, bf16[512,1024]{1,0:T(8,128)(2,1)}), (bf16[512,2048]{1,0:T(8,128)(2,1)}, bf16[512,1024]{1,0:T(8,128)(2,1)})) %all-reduce.3.cloned.1.call-update) | async-done | bytes 3145744 | tf_op jit(solution)/shard_map/psum | solution.py:68
  304.1 2.2 convert_element_type.51
  306.3 1.5 fusion.2
  307.9 3.4 fusion.12
  312.3 9.1 %all-to-all-start.3 = ((bf16[64,8,448]{2,1,0:T(8,128)(2,1)}), bf16[64,8,448]{2,1,0:T(8,128)(2,1)S(1)}, u32[]{:S(2)}, u32[]{:S(2)}) async-start(bf16[64,8,448]{2,1,0:T(8,128)(2,1)} %bitcast.45), calls=%async_computation.3 | async-start | bytes 1048576 | tf_op jit(solution)/shard_map/all_to_all | solution.py:89
  321.4 2.5 convolution_convert_fusion.3
  324.9 14.4 %all-to-all-done.3 = bf16[64,8,448]{2,1,0:T(8,128)(2,1)S(1)} async-done(((bf16[64,8,448]{2,1,0:T(8,128)(2,1)}), bf16[64,8,448]{2,1,0:T(8,128)(2,1)S(1)}, u32[]{:S(2)}, u32[]{:S(2)}) %all-to-all-start.3) | async-done | bytes 458784 | tf_op jit(solution)/shard_map/all_to_all | solution.py:89
  339.3 4.6 %all-to-all-start.1 = ((bf16[64,8,448]{2,1,0:T(8,128)(2,1)}), bf16[64,8,448]{2,1,0:T(8,128)(2,1)S(1)}, u32[]{:S(2)}, u32[]{:S(2)}) async-start(bf16[64,8,448]{2,1,0:T(8,128)(2,1)} %bitcast.41), calls=%async_computation.1 | async-start | bytes 1048576 | tf_op jit(solution)/shard_map/all_to_all | solution.py:74
  344.0 1.6 fusion.11
  345.6 1.2 gather_fusion.1
  348.4 13.5 %all-to-all-done.1 = bf16[64,8,448]{2,1,0:T(8,128)(2,1)S(1)} async-done(((bf16[64,8,448]{2,1,0:T(8,128)(2,1)}), bf16[64,8,448]{2,1,0:T(8,128)(2,1)S(1)}, u32[]{:S(2)}, u32[]{:S(2)}) %all-to-all-start.1) | async-done | bytes 458784 | tf_op jit(solution)/shard_map/all_to_all | solution.py:74
  361.8 1.2 gather_fusion
  (49 shorter events, 13.8 us)
Async XLA Ops:
  32.7 21.1 %copy-start.1 = (bf16[128,448]{0,1:T(8,128)(2,1)S(1)}, bf16[128,448]{0,1:T(8,128)(2,1)}, u32[]{:S(2)}) copy-start(bf16[128,448]{0,1:T(8,128)(2,1)} %param.7) | copy-start | bytes 344068
  36.7 30.1 %all-to-all-start.2 = ((bf16[64,8,448]{2,1,0:T(8,128)(2,1)}), bf16[64,8,448]{2,1,0:T(8,128)(2,1)S(1)}, u32[]{:S(2)}, u32[]{:S(2)}) async-start(bf16[64,8,448]{2,1,0:T(8,128)(2,1)} %bitcast.43), calls=%async_computation.2 | async-start | bytes 1048576 | tf_op jit(solution)/shard_map/all_to_all | solution.py:54
  49.2 78.4 %collective-permute-start = (bf16[1,448,2048]{2,1,0:T(8,128)(2,1)}, bf16[1,448,2048]{2,1,0:T(8,128)(2,1)}, u32[]{:S(2)}, u32[]{:S(2)}) collective-permute-start(bf16[1,448,2048]{2,1,0:T(8,128)(2,1)} %param.9), channel_id=1, source_target_pairs={{32,0},{33,1},{34,2},{35,3},{36,4},{37,5},{38,6},{39,7},{40,8},{41... | collective-permute-start | bytes 5505032 | tf_op jit(solution)/shard_map/ppermute | solution.py:10
  66.8 60.8 %all-to-all-start = ((bf16[64,8,448]{2,1,0:T(8,128)(2,1)}), bf16[64,8,448]{2,1,0:T(8,128)(2,1)S(1)}, u32[]{:S(2)}, u32[]{:S(2)}) async-start(bf16[64,8,448]{2,1,0:T(8,128)(2,1)} %bitcast.36), calls=%async_computation | async-start | bytes 1048576 | tf_op jit(solution)/shard_map/all_to_all | solution.py:47
  71.8 55.9 %copy-start.2 = (bf16[1,448,2048]{2,1,0:T(8,128)(2,1)S(1)}, bf16[1,448,2048]{2,1,0:T(8,128)(2,1)}, u32[]{:S(2)}) copy-start(bf16[1,448,2048]{2,1,0:T(8,128)(2,1)} %param.9) | copy-start | bytes 5505028
  71.8 232.3 %all-reduce.3.cloned.1.call-start = ((), (), s32[]{:S(2)}) async-start(), calls=%async_computation.4 | async-start | bytes 6291456 | tf_op jit(solution)/shard_map/psum | solution.py:68
  71.8 52.5 %collective-permute-start.1 = (bf16[1,1024,448]{1,2,0:T(8,128)(2,1)}, bf16[1,1024,448]{1,2,0:T(8,128)(2,1)S(1)}, u32[]{:S(2)}, u32[]{:S(2)}) collective-permute-start(bf16[1,1024,448]{1,2,0:T(8,128)(2,1)} %param.10), channel_id=1, source_target_pairs={{32,0},{33,1},{34,2},{35,3},{36,4},{37,5},{38,6},{39,7},{40,8},{41... | collective-permute-start | bytes 2752520 | tf_op jit(solution)/shard_map/ppermute | solution.py:10
  124.3 0.9 copy-start.5
  304.1 2.2 copy-start
  306.3 1.5 copy-start.3
  307.8 13.5 %copy-start.4 = (bf16[1,1024,448]{1,2,0:T(8,128)(2,1)S(1)}, bf16[1,1024,448]{1,2,0:T(8,128)(2,1)}, u32[]{:S(2)}) copy-start(bf16[1,1024,448]{1,2,0:T(8,128)(2,1)} %param.10) | copy-start | bytes 2752516
  312.3 27.1 %all-to-all-start.3 = ((bf16[64,8,448]{2,1,0:T(8,128)(2,1)}), bf16[64,8,448]{2,1,0:T(8,128)(2,1)S(1)}, u32[]{:S(2)}, u32[]{:S(2)}) async-start(bf16[64,8,448]{2,1,0:T(8,128)(2,1)} %bitcast.45), calls=%async_computation.3 | async-start | bytes 1048576 | tf_op jit(solution)/shard_map/all_to_all | solution.py:89
  339.3 22.5 %all-to-all-start.1 = ((bf16[64,8,448]{2,1,0:T(8,128)(2,1)}), bf16[64,8,448]{2,1,0:T(8,128)(2,1)S(1)}, u32[]{:S(2)}, u32[]{:S(2)}) async-start(bf16[64,8,448]{2,1,0:T(8,128)(2,1)} %bitcast.41), calls=%async_computation.1 | async-start | bytes 1048576 | tf_op jit(solution)/shard_map/all_to_all | solution.py:74
Sparse Core Ops, SparseCore 0:
  132.6 171.4 all-reduce.2
where the time goes:
time: 373 us; the launch traced here: 372 us
  waiting for transfers between devices  257 us (69%)
  starting transfers between devices  40.6 us (11%)
  other arithmetic  29.2 us (8%)
  local copies, waits for them, and re-layouts  15.4 us (4%)
  matrix products  14.7 us (4%)
  between operations  14.3 us (4%)
    psum x1, waiting for transfers between devices, on_device(): lax.psum(gate_up_part.astype(jnp.bfloat16), 'dp').astype(jnp.float32)  172 us
    ppermute x2, waiting for transfers between devices, shifted(): return lax.ppermute(block, axis, route)  47.6 us
    select_n x2, other arithmetic, on_device(): target = jnp.where(moved[flat % half], (flat + half) % experts, flat)  15.6 us
    all_to_all x1, waiting for transfers between devices, on_device(): lax.all_to_all(row_dx, 'expert', split_axis=0, concat_axis=0, tiled=True)  14.4 us
    all_to_all x1, waiting for transfers between devices, on_device(): lax.all_to_all(row_out, 'expert', split_axis=0, concat_axis=0, tiled=True)  13.5 us
    all_to_all x1, starting transfers between devices, on_device(): lax.all_to_all(send_grads.reshape(experts, capacity, width_block), 'exper...  12.5 us
    all_to_all x1, waiting for transfers between devices, on_device(): lax.all_to_all(send_grads.reshape(experts, capacity, width_block), 'exper...  10.3 us
    ppermute x2, starting transfers between devices, shifted(): return lax.ppermute(block, axis, route)  9.36 us
  transfers between devices with their start and end apart: 7, of which 5 were waited for; matrix products, arithmetic and copies ran while one was open for 4% of the time, Pallas kernels for 0%

commit v1 on v0

v1 whole, which is shorter than its diff:
```python
import functools

import jax
import jax.numpy as jnp
from jax import lax
from jax.experimental import pallas as pl
from jax.experimental.pallas import tpu as pltpu
from jax.sharding import PartitionSpec as P

MESH = pl.DeviceIdType.MESH
F32 = jnp.float32
BF16 = jnp.bfloat16
SEMS = 80


def dot(a, b, dims):
    return lax.dot_general(a, b, (dims, ((), ())), preferred_element_type=F32)


def kernel(
    experts, cap,
    tok_ref, grad_ref, wg_hbm, wd_hbm, routes_ref, rw_ref, swapped_ref,
    out_ref, dx_ref, dg_hbm,
    wp, wd, st, sg, rt, rg, so, sx, ro, rx, tm, gm, pt,
    pg, xg, sgu, relg, augg, fromg, own,
    ph, xh, sh, relh, augh, fromh,
    hf, gu, eg, er, ed,
    ss, rs, lsem,
):
    dp = lax.axis_index("dp")
    me = lax.axis_index("expert")
    h, c = dp // 2, dp % 2
    tokens, width = tok_ref.shape
    rows = experts * cap
    half = rows // 2
    units = wd.shape[0] // 8
    plus = {"dp": lax.rem(dp + 2, 8)}
    minus = {"dp": lax.rem(dp + 6, 8)}
    other = {"dp": 2 * h + 1 - c}
    top, low = pl.ds(0, half), pl.ds(half, half)

    barrier = pltpu.get_barrier_semaphore()

    def greet(k, carry):
        pl.semaphore_signal(
            barrier, inc=1, device_id={"expert": lax.rem(me + k, experts)}, device_id_type=MESH
        )
        return carry

    for peer in (plus, minus, other):
        pl.semaphore_signal(barrier, inc=1, device_id=peer, device_id_type=MESH)
    lax.fori_loop(1, experts, greet, 0)

    loads = [pltpu.make_async_copy(wd_hbm.at[0], wd, lsem.at[0])]
    for u in range(8):
        for part in range(2):
            loads.append(
                pltpu.make_async_copy(
                    wg_hbm.at[0, :, pl.ds((8 * part + u) * units, units)],
                    wp.at[:, pl.ds((2 * u + part) * units, units)],
                    lsem.at[1 + 2 * u + part],
                )
            )
    for load in loads:
        load.start()

    def remote(src, dst, i, device):
        return pltpu.make_async_remote_copy(
            src_ref=src, dst_ref=dst, send_sem=ss.at[i], recv_sem=rs.at[i],
            device_id=device, device_id_type=MESH,
        )

    def exchange(src, dst, i):
        pltpu.make_async_copy(src.at[me], dst.at[me], rs.at[i]).start()

        def send(k, carry):
            peer = lax.rem(me + k, experts)
            remote(src.at[peer], dst.at[me], i, {"expert": peer}).start()
            return carry

        lax.fori_loop(1, experts, send, 0)

    def arrived(dst, i):
        pltpu.make_async_copy(dst, dst, rs.at[i]).wait()

    def departed(src, i):
        part = src.at[pl.ds(0, experts - 1)]
        remote(part, part, i, {"expert": me}).wait_send()

    lanes = lax.broadcasted_iota(jnp.int32, (tokens, experts), 1)
    named = [jnp.where(routes_ref[:, k : k + 1] == lanes, 1.0, 0.0).astype(BF16) for k in range(2)]
    before = (
        lax.broadcasted_iota(jnp.int32, (tokens, tokens), 1)
        < lax.broadcasted_iota(jnp.int32, (tokens, tokens), 0)
    )
    before = jnp.where(before, 1.0, 0.0).astype(BF16)
    counts = [dot(before, n, ((1,), (0,))) for n in named]
    counts[1] = counts[1] + jnp.sum(named[0].astype(F32), axis=0, keepdims=True)
    places = lax.broadcasted_iota(jnp.int32, (tokens, rows), 1)
    for k in range(2):
        slot = jnp.sum(named[k].astype(F32) * counts[k], axis=1, keepdims=True).astype(jnp.int32)
        spot = routes_ref[:, k : k + 1] * cap + slot
        pt[pl.ds(k * tokens, tokens), :] = jnp.where(spot == places, 1.0, 0.0).astype(BF16)
    both = pt[pl.ds(0, tokens), :] + pt[pl.ds(tokens, tokens), :]
    st[...] = dot(both, tok_ref[...], ((0,), (0,))).reshape(experts, cap, width).astype(BF16)
    pl.semaphore_wait(barrier, experts + 2)
    exchange(st, rt, 0)
    grad = grad_ref[...].astype(F32)
    weighted = jnp.concatenate(
        [(rw_ref[:, k : k + 1] * grad).astype(BF16) for k in range(2)], axis=0
    )
    sg[...] = dot(pt[...], weighted, ((0,), (0,))).reshape(experts, cap, width).astype(BF16)
    exchange(sg, rg, 1)

    def reduce_parts(left, parts, xrecv, sums, rel, frm, base, right, dims, w):
        swaps = {}
        for d in (2, 1, 3, 0):
            j = lax.rem(h + d, 4)
            block = dot(left[...], right(j), dims).astype(BF16)
            parts[d, 0] = block[:, :w]
            parts[d, 1] = block[:, w:]
            swaps[d] = remote(parts.at[d, 1 - c], xrecv.at[d], base + d, other)
            swaps[d].start()
        sent = list(swaps.values())
        for d in (2, 1, 3, 0):
            swaps[d].wait_recv()
            sums[d] = (parts[d, c].astype(F32) + xrecv[d].astype(F32)).astype(BF16)
            if d == 2:
                new = [
                    remote(sums.at[2, top], rel.at[0], base + 4, plus),
                    remote(sums.at[2, low], rel.at[1], base + 5, minus),
                ]
            elif d == 1:
                new = [remote(sums.at[1, low], frm.at[0, low], base + 6, plus)]
            elif d == 3:
                new = [remote(sums.at[3, top], frm.at[1, top], base + 7, minus)]
            else:
                new = []
            for copy in new:
                copy.start()
            sent += new
        return sent

    def reduce_relay(sums, rel, aug, frm, base):
        remote(rel.at[0], rel.at[0], base + 4, plus).wait_recv()
        aug[0] = (sums[1, top].astype(F32) + rel[0].astype(F32)).astype(BF16)
        one = remote(aug.at[0], frm.at[0, top], base + 8, plus)
        one.start()
        remote(rel.at[1], rel.at[1], base + 5, minus).wait_recv()
        aug[1] = (sums[3, low].astype(F32) + rel[1].astype(F32)).astype(BF16)
        two = remote(aug.at[1], frm.at[1, low], base + 9, minus)
        two.start()
        return [one, two]

    def reduce_end(sums, frm, base):
        remote(frm.at[0, low], frm.at[0, low], base + 6, plus).wait_recv()
        remote(frm.at[1, top], frm.at[1, top], base + 7, minus).wait_recv()
        remote(frm.at[0, top], frm.at[0, top], base + 8, plus).wait_recv()
        remote(frm.at[1, low], frm.at[1, low], base + 9, minus).wait_recv()
        return sums[0].astype(F32) + frm[0].astype(F32) + frm[1].astype(F32)

    def block_of(index, w):
        return pl.ds(pl.multiple_of(index * w, w), w)

    u_own = 2 * h + c
    u_plus = 2 * lax.rem(h + 1, 4) + c
    u_minus = 2 * lax.rem(h + 3, 4) + c
    u_far = 2 * lax.rem(h + 2, 4) + c

    def gather_start(buf, w, base):
        mine = block_of(u_own, w)
        new = [
            remote(buf.at[top, mine], buf.at[top, mine], base + 0, plus),
            remote(buf.at[low, mine], buf.at[low, mine], base + 1, minus),
            remote(buf.at[low, mine], buf.at[low, mine], base + 2, plus),
            remote(buf.at[top, mine], buf.at[top, mine], base + 3, minus),
            remote(buf.at[:, mine], buf.at[:, mine], base + 6, other),
        ]
        for copy in new:
            copy.start()
        return new

    def gather_relay(buf, w, base):
        new = []

        def on(rows_of, u, i, device, onward, over):
            ref = buf.at[rows_of, block_of(u, w)]
            remote(ref, ref, base + i, device).wait_recv()
            if onward is not None:
                new.append(remote(ref, ref, base + onward, device))
                new[-1].start()
            new.append(remote(ref, ref, base + over, other))
            new[-1].start()

        on(top, u_minus, 0, plus, 4, 7)
        on(low, u_plus, 1, minus, 5, 8)
        on(low, u_minus, 2, plus, None, 9)
        on(top, u_plus, 3, minus, None, 10)
        return new, on

    def gather_end(buf, w, base, on):
        on(top, u_far, 4, plus, None, 11)
        on(low, u_far, 5, minus, None, 12)
        shift = 1 - 2 * c
        for rows_of, u, i in (
            (slice(None), u_own, 6), (top, u_minus, 7), (low, u_plus, 8), (low, u_minus, 9),
            (top, u_plus, 10), (top, u_far, 11), (low, u_far, 12),
        ):
            ref = buf.at[rows_of, block_of(u + shift, w)]
            remote(ref, ref, base + i, other).wait_recv()

    sent = []
    arrived(rt, 0)
    tm[...] = rt[...].astype(F32).reshape(rows, width).astype(BF16)
    for load in loads:
        load.wait()
    RG, RH, AH, AG = 4, 14, 24, 37
    sent += reduce_parts(
        tm, pg, xg, sgu, relg, fromg, RG,
        lambda j: wp[:, pl.ds(pl.multiple_of(4 * units * j, 4 * units), 4 * units)],
        ((1,), (0,)), 2 * units,
    )
    arrived(rg, 1)
    gm[...] = rg[...].astype(F32).reshape(rows, width).astype(BF16)
    sent += reduce_parts(
        gm, ph, xh, sh, relh, fromh, RH,
        lambda j: wd[pl.ds(pl.multiple_of(2 * units * j, 2 * units), 2 * units), :],
        ((1,), (1,)), units,
    )
    sent += reduce_relay(sgu, relg, augg, fromg, RG)
    sent += reduce_relay(sh, relh, augh, fromh, RH)
    own[...] = reduce_end(sgu, fromg, RG)
    gate, up = own[:, :units], own[:, units:]
    hf[:, block_of(u_own, units)] = (gate * jax.nn.sigmoid(gate) * up).astype(BF16)
    sent += gather_start(hf, units, AH)
    hidden_grad = reduce_end(sh, fromh, RH)
    gate, up = own[:, :units], own[:, units:]
    sig = jax.nn.sigmoid(gate)
    gate_grad = hidden_grad * up * sig * (1.0 + gate * (1.0 - sig))
    up_grad = hidden_grad * (gate * sig)
    gu[:, block_of(u_own, 2 * units)] = jnp.concatenate([gate_grad, up_grad], axis=1).astype(BF16)
    sent += gather_start(gu, 2 * units, AG)
    new, on = gather_relay(hf, units, AH)
    gather_end(hf, units, AH, on)
    sent += new
    so[...] = dot(hf[...], wd[...], ((1,), (0,))).reshape(experts, cap, width).astype(BF16)
    exchange(so, ro, 2)
    eg[...] = dot(hf[...], gm[...], ((0,), (0,))).astype(BF16)
    trade = remote(eg, er, 50, {"expert": lax.rem(me + experts // 2, experts)})
    trade.start()
    new, on = gather_relay(gu, 2 * units, AG)
    gather_end(gu, 2 * units, AG, on)
    sent += new
    sx[...] = dot(gu[...], wp[...], ((1,), (1,))).reshape(experts, cap, width).astype(BF16)
    exchange(sx, rx, 3)
    trade.wait_recv()
    moved = jnp.where(swapped_ref[...] == lax.rem(me, experts // 2), 1.0, 0.0)
    moved = jnp.max(moved, axis=1, keepdims=True)
    ed[...] = jnp.where(moved > 0.5, er[...].astype(F32), eg[...].astype(F32)).astype(BF16)
    store = pltpu.make_async_copy(ed, dg_hbm.at[0], lsem.at[0])
    store.start()
    arrived(ro, 2)
    back = ro[...].astype(F32).reshape(rows, width).astype(BF16)
    total = rw_ref[:, 0:1] * dot(pt[pl.ds(0, tokens), :], back, ((1,), (0,)))
    total = total + rw_ref[:, 1:2] * dot(pt[pl.ds(tokens, tokens), :], back, ((1,), (0,)))
    out_ref[...] = total.astype(BF16)
    arrived(rx, 3)
    both = pt[pl.ds(0, tokens), :] + pt[pl.ds(tokens, tokens), :]
    back = rx[...].astype(F32).reshape(rows, width).astype(BF16)
    dx_ref[...] = dot(both, back, ((1,), (0,))).astype(BF16)
    for copy in sent:
        copy.wait_send()
    trade.wait_send()
    departed(st, 0)
    departed(sg, 1)
    departed(so, 2)
    departed(sx, 3)
    store.wait()


def on_device(tokens, out_grad, gate_up_weight, down_weight, routes, route_weight, swapped):
    experts = lax.axis_size("expert")
    count, width = tokens.shape
    hidden = down_weight.shape[1]
    cap = max(2, 2 * count * routes.shape[1] // experts)
    rows = experts * cap
    units = hidden // 8
    half = rows // 2
    vm = lambda *shape: pltpu.VMEM(shape, BF16)
    scratch = [
        vm(width, 2 * hidden), vm(hidden, width),
        *[vm(experts, cap, width) for _ in range(8)],
        vm(rows, width), vm(rows, width), vm(2 * count, rows),
        vm(4, 2, rows, 2 * units), vm(4, rows, 2 * units), vm(4, rows, 2 * units),
        vm(2, half, 2 * units), vm(2, half, 2 * units), vm(2, rows, 2 * units),
        pltpu.VMEM((rows, 2 * units), F32),
        vm(4, 2, rows, units), vm(4, rows, units), vm(4, rows, units),
        vm(2, half, units), vm(2, half, units), vm(2, rows, units),
        vm(rows, hidden), vm(rows, 2 * hidden),
        vm(hidden, width), vm(hidden, width), vm(hidden, width),
        pltpu.SemaphoreType.DMA((SEMS,)), pltpu.SemaphoreType.DMA((SEMS,)),
        pltpu.SemaphoreType.DMA((17,)),
    ]
    whole = pl.BlockSpec(memory_space=pltpu.VMEM)
    place = pl.BlockSpec(memory_space=pl.ANY)
    return pl.pallas_call(
        functools.partial(kernel, experts, cap),
        out_shape=(
            jax.ShapeDtypeStruct((count, width), BF16),
            jax.ShapeDtypeStruct((count, width), BF16),
            jax.ShapeDtypeStruct(down_weight.shape, BF16),
        ),
        in_specs=[whole, whole, place, place, whole, whole, whole],
        out_specs=(whole, whole, place),
        scratch_shapes=scratch,
        compiler_params=pltpu.CompilerParams(collective_id=0, has_side_effects=True),
        name="layer",
    )(tokens, out_grad, gate_up_weight, down_weight, routes, route_weight, swapped.reshape(1, -1))


def solution(mesh):
    return jax.shard_map(
        on_device,
        mesh=mesh,
        in_specs=(
            P("expert", "dp"),
            P("expert", "dp"),
            P("expert", "dp", None),
            P("expert", None, "dp"),
            P("expert", None),
            P("expert", None),
            P(),
        ),
        out_specs=(P("expert", "dp"), P("expert", "dp"), P("expert", None, "dp")),
        check_vma=False,
    )
```

time: 373 us -> 193 us (0.52)
  waiting for transfers between devices: 257 us -> 0 us
  Pallas kernels: 0 us -> 176 us
  starting transfers between devices: 40.6 us -> 0 us
  other arithmetic: 29.2 us -> 0 us
  matrix products: 14.7 us -> 0 us
  between operations: 14.3 us -> 0.64 us
    pallas_call x0 -> x1, Pallas kernels: none -> 176 us  [on_device(): pl.pallas_call(functools.partial(kernel, experts, cap), out_shape=(jax.Sh...]
    psum x1 -> x0, waiting for transfers between devices: 172 us -> none  [on_device(): lax.psum(gate_up_part.astype(jnp.bfloat16), 'dp').astype(jnp.float32)]
    ppermute x2 -> x0, waiting for transfers between devices: 47.6 us -> none  [shifted(): return lax.ppermute(block, axis, route)]
    all_to_all x4 -> x0, waiting for transfers between devices: 38.2 us -> none  [the longest x1 14.4 us: on_device(): lax.all_to_all(row_dx, 'expert', split_axis=0, concat_axis=0, tiled=True)]
    all_to_all x4 -> x0, starting transfers between devices: 31.2 us -> none  [the longest x1 12.5 us: on_device(): lax.all_to_all(send_grads.reshape(experts, capacity, width_block), 'exper...]
    select_n x3 -> x0, other arithmetic: 15.7 us -> none  [the longest x2 15.6 us: on_device(): target = jnp.where(moved[flat % half], (flat + half) % experts, flat)]
    dot_general x5 -> x0, matrix products: 14.7 us -> none  [the longest x1 4.77 us: on_device(): jnp.dot(recv_tokens, local_gate_up, preferred_element_type=jnp.float32)]
    ppermute x2 -> x0, starting transfers between devices: 9.36 us -> none  [shifted(): return lax.ppermute(block, axis, route)]
  transfers between devices with their start and end apart: 7 -> 0, of which waited for: 5 -> 0; matrix products, arithmetic and copies ran while one was open for 4% -> 0% of each run, Pallas kernels for 0% -> 0%
where the time goes in v1:
time: 193 us; the launch traced here: 191 us
  Pallas kernels  176 us (91%)
  local copies, waits for them, and re-layouts  14 us (7%)
    pallas_call x1, Pallas kernels, on_device(): pl.pallas_call(functools.partial(kernel, experts, cap), out_shape=(jax.Sh...  176 us
    unnamed x5, local copies, waits for them, and re-layouts  8.41 us
    pallas_call x3, local copies, waits for them, and re-layouts, on_device(): pl.pallas_call(functools.partial(kernel, experts, cap), out_shape=(jax.Sh...  5.55 us

profile of v1, /device:TPU:1, one launch (start us, length us, event | category | flops | bytes accessed | tf_op | source)
XLA Modules:
  0.0 190.7 jit_solution(1881364891012732997)
XLA Ops:
  0.6 1.4 copy.13.routes_ref
  2.0 1.4 copy.14.rw_ref
  3.5 1.7 copy.10.tok_ref
  5.1 1.7 copy.11.grad_ref
  6.8 2.3 %copy.12.wd_hbm = bf16[1,1024,448]{2,1,0:T(8,128)(2,1)} copy(bf16[1,1024,448]{1,2,0:T(8,128)(2,1)} %param.10) | data formatting | bytes 1835008 | tf_op args[3]
  9.0 176.1 %layer.1 = (bf16[128,448]{1,0:T(8,128)(2,1)}, bf16[128,448]{1,0:T(8,128)(2,1)}, bf16[1,1024,448]{2,1,0:T(8,128)(2,1)}) custom-call(bf16[128,448]{1,0:T(8,128)(2,1)} %copy.10.tok_ref, bf16[128,448]{1,0:T(8,128)(2,1)} %copy.11.grad_ref, bf16[1,448,2048]{2,1,0:T(8,128)(2,1)} %wg_hbm.1, bf16[1,1024,448]{2,1,0:T(8,128)(2,1)} %copy.12.wd_hbm, ...), custom_call_target="tpu_custom_call" | custom-call | tf_op jit(solution)/shard_map/layer/pallas_call | solution.py:306
  185.1 1.7 copy.15
  186.8 1.7 copy.16
  188.5 2.2 %copy.17 = bf16[1,1024,448]{1,2,0:T(8,128)(2,1)} copy(bf16[1,1024,448]{2,1,0:T(8,128)(2,1)} %get-tuple-element.5) | data formatting | bytes 1835008 | tf_op jit(solution)/shard_map/layer/pallas_call | solution.py:306

commit v2 on v1

--- a/solution.py
+++ b/solution.py
@@ -19,9 +19,10 @@
 
 def kernel(
     experts, cap,
-    tok_ref, grad_ref, wg_hbm, wd_hbm, routes_ref, rw_ref, swapped_ref,
+    tok_hbm, grad_hbm, wg_hbm, wd_hbm, routes_hbm, rw_hbm, swapped_hbm,
     out_ref, dx_ref, dg_hbm,
-    wp, wd, st, sg, rt, rg, so, sx, ro, rx, tm, gm, pt,
+    tok_ref, grad_ref, routes_ref, rw_ref, swapped_ref,
+    wp, wd, xt, st, sg, rt, rg, so, sx, ro, rx, tm, gm, sel,
     pg, xg, sgu, relg, augg, fromg, own,
     ph, xh, sh, relh, augh, fromh,
     hf, gu, eg, er, ed,
@@ -30,10 +31,12 @@
     dp = lax.axis_index("dp")
     me = lax.axis_index("expert")
     h, c = dp // 2, dp % 2
-    tokens, width = tok_ref.shape
+    width, tokens = tok_ref.shape
+    body = width // 128 * 128
+    rest = width - body
     rows = experts * cap
     half = rows // 2
-    units = wd.shape[0] // 8
+    units = wd.shape[1] // 8
     plus = {"dp": lax.rem(dp + 2, 8)}
     minus = {"dp": lax.rem(dp + 6, 8)}
     other = {"dp": 2 * h + 1 - c}
@@ -51,6 +54,15 @@
         pl.semaphore_signal(barrier, inc=1, device_id=peer, device_id_type=MESH)
     lax.fori_loop(1, experts, greet, 0)
 
+    small = [
+        pltpu.make_async_copy(src, dst, lsem.at[17 + i])
+        for i, (src, dst) in enumerate((
+            (routes_hbm, routes_ref), (tok_hbm, tok_ref), (grad_hbm, grad_ref), (rw_hbm, rw_ref),
+            (swapped_hbm, swapped_ref),
+        ))
+    ]
+    for load in small:
+        load.start()
     loads = [pltpu.make_async_copy(wd_hbm.at[0], wd, lsem.at[0])]
     for u in range(8):
         for part in range(2):
@@ -87,29 +99,33 @@
         part = src.at[pl.ds(0, experts - 1)]
         remote(part, part, i, {"expert": me}).wait_send()
 
-    lanes = lax.broadcasted_iota(jnp.int32, (tokens, experts), 1)
-    named = [jnp.where(routes_ref[:, k : k + 1] == lanes, 1.0, 0.0).astype(BF16) for k in range(2)]
+    for load in small:
+        load.wait()
+    ids = lax.broadcasted_iota(jnp.int32, (experts, tokens), 0)
+    named = [jnp.where(routes_ref[k : k + 1, :] == ids, 1.0, 0.0) for k in range(2)]
     before = (
-        lax.broadcasted_iota(jnp.int32, (tokens, tokens), 1)
-        < lax.broadcasted_iota(jnp.int32, (tokens, tokens), 0)
+        lax.broadcasted_iota(jnp.int32, (tokens, tokens), 0)
+        < lax.broadcasted_iota(jnp.int32, (tokens, tokens), 1)
     )
     before = jnp.where(before, 1.0, 0.0).astype(BF16)
-    counts = [dot(before, n, ((1,), (0,))) for n in named]
-    counts[1] = counts[1] + jnp.sum(named[0].astype(F32), axis=0, keepdims=True)
-    places = lax.broadcasted_iota(jnp.int32, (tokens, rows), 1)
+    counts = [dot(n.astype(BF16), before, ((1,), (0,))) for n in named]
+    counts[1] = counts[1] + jnp.sum(named[0], axis=1, keepdims=True)
+    places = lax.broadcasted_iota(jnp.int32, (rows, tokens), 0)
+    grad = grad_ref[...].astype(F32)
     for k in range(2):
-        slot = jnp.sum(named[k].astype(F32) * counts[k], axis=1, keepdims=True).astype(jnp.int32)
-        spot = routes_ref[:, k : k + 1] * cap + slot
-        pt[pl.ds(k * tokens, tokens), :] = jnp.where(spot == places, 1.0, 0.0).astype(BF16)
-    both = pt[pl.ds(0, tokens), :] + pt[pl.ds(tokens, tokens), :]
-    st[...] = dot(both, tok_ref[...], ((0,), (0,))).reshape(experts, cap, width).astype(BF16)
+        of = pl.ds(k * tokens, tokens)
+        slot = jnp.sum(named[k] * counts[k], axis=0, keepdims=True).astype(jnp.int32)
+        spot = routes_ref[k : k + 1, :] * cap + slot
+        sel[:, of] = jnp.where(spot == places, 1.0, 0.0).astype(BF16)
+        xt[pl.ds(0, width), of] = tok_ref[...]
+        weighted = (rw_ref[k : k + 1, :] * grad).astype(BF16)
+        xt[pl.ds(width, rest), of] = weighted[body:]
+        xt[pl.ds(width + rest, body), of] = weighted[:body]
+    full = width + rest
+    st[...] = dot(sel[...], xt[pl.ds(0, full), :], ((1,), (1,))).reshape(experts, cap, full).astype(BF16)
     pl.semaphore_wait(barrier, experts + 2)
     exchange(st, rt, 0)
-    grad = grad_ref[...].astype(F32)
-    weighted = jnp.concatenate(
-        [(rw_ref[:, k : k + 1] * grad).astype(BF16) for k in range(2)], axis=0
-    )
-    sg[...] = dot(pt[...], weighted, ((0,), (0,))).reshape(experts, cap, width).astype(BF16)
+    sg[...] = dot(sel[...], xt[pl.ds(full, body), :], ((1,), (1,))).reshape(experts, cap, body).astype(BF16)
     exchange(sg, rg, 1)
 
     def reduce_parts(left, parts, xrecv, sums, rel, frm, base, right, dims, w):
@@ -167,40 +183,35 @@
     u_minus = 2 * lax.rem(h + 3, 4) + c
     u_far = 2 * lax.rem(h + 2, 4) + c
 
-    def gather_start(buf, w, base):
+    def put(sent, src, dst, i, device):
+        copy = remote(src, dst, i, device)
+        copy.start()
+        sent.append(copy)
+
+    def gather_first(sent, buf, w, base):
         mine = block_of(u_own, w)
-        new = [
-            remote(buf.at[top, mine], buf.at[top, mine], base + 0, plus),
-            remote(buf.at[low, mine], buf.at[low, mine], base + 1, minus),
-            remote(buf.at[low, mine], buf.at[low, mine], base + 2, plus),
-            remote(buf.at[top, mine], buf.at[top, mine], base + 3, minus),
-            remote(buf.at[:, mine], buf.at[:, mine], base + 6, other),
-        ]
-        for copy in new:
-            copy.start()
-        return new
-
-    def gather_relay(buf, w, base):
-        new = []
-
-        def on(rows_of, u, i, device, onward, over):
+        put(sent, buf.at[top, mine], buf.at[top, mine], base + 0, plus)
+        put(sent, buf.at[low, mine], buf.at[low, mine], base + 1, minus)
+
+    def gather_second(sent, buf, w, base):
+        mine = block_of(u_own, w)
+        put(sent, buf.at[low, mine], buf.at[low, mine], base + 2, plus)
+        put(sent, buf.at[top, mine], buf.at[top, mine], base + 3, minus)
+        put(sent, buf.at[:, mine], buf.at[:, mine], base + 6, other)
+
+    def gather_on(sent, buf, w, base, steps):
+        for rows_of, u, i, device, onward, over in steps:
             ref = buf.at[rows_of, block_of(u, w)]
             remote(ref, ref, base + i, device).wait_recv()
             if onward is not None:
-                new.append(remote(ref, ref, base + onward, device))
-                new[-1].start()
-            new.append(remote(ref, ref, base + over, other))
-            new[-1].start()
-
-        on(top, u_minus, 0, plus, 4, 7)
-        on(low, u_plus, 1, minus, 5, 8)
-        on(low, u_minus, 2, plus, None, 9)
-        on(top, u_plus, 3, minus, None, 10)
-        return new, on
-
-    def gather_end(buf, w, base, on):
-        on(top, u_far, 4, plus, None, 11)
-        on(low, u_far, 5, minus, None, 12)
+                put(sent, ref, ref, base + onward, device)
+            put(sent, ref, ref, base + over, other)
+
+    on_first = ((top, u_minus, 0, plus, 4, 7), (low, u_plus, 1, minus, 5, 8))
+    on_second = ((low, u_minus, 2, plus, None, 9), (top, u_plus, 3, minus, None, 10))
+    on_last = ((top, u_far, 4, plus, None, 11), (low, u_far, 5, minus, None, 12))
+
+    def gather_end(buf, w, base):
         shift = 1 - 2 * c
         for rows_of, u, i in (
             (slice(None), u_own, 6), (top, u_minus, 7), (low, u_plus, 8), (low, u_minus, 9),
@@ -211,7 +222,9 @@
 
     sent = []
     arrived(rt, 0)
-    tm[...] = rt[...].astype(F32).reshape(rows, width).astype(BF16)
+    came = rt[...].astype(F32).reshape(rows, full)
+    tm[...] = came[:, :width].astype(BF16)
+    gm[:, body:] = came[:, width:].astype(BF16)
     for load in loads:
         load.wait()
     RG, RH, AH, AG = 4, 14, 24, 37
@@ -221,37 +234,43 @@
         ((1,), (0,)), 2 * units,
     )
     arrived(rg, 1)
-    gm[...] = rg[...].astype(F32).reshape(rows, width).astype(BF16)
+    gm[:, :body] = rg[...].astype(F32).reshape(rows, body).astype(BF16)
     sent += reduce_parts(
         gm, ph, xh, sh, relh, fromh, RH,
-        lambda j: wd[pl.ds(pl.multiple_of(2 * units * j, 2 * units), 2 * units), :],
-        ((1,), (1,)), units,
+        lambda j: wd[:, pl.ds(pl.multiple_of(2 * units * j, 2 * units), 2 * units)],
+        ((1,), (0,)), units,
     )
     sent += reduce_relay(sgu, relg, augg, fromg, RG)
     sent += reduce_relay(sh, relh, augh, fromh, RH)
     own[...] = reduce_end(sgu, fromg, RG)
     gate, up = own[:, :units], own[:, units:]
     hf[:, block_of(u_own, units)] = (gate * jax.nn.sigmoid(gate) * up).astype(BF16)
-    sent += gather_start(hf, units, AH)
+    gather_first(sent, hf, units, AH)
+    gather_second(sent, hf, units, AH)
     hidden_grad = reduce_end(sh, fromh, RH)
     gate, up = own[:, :units], own[:, units:]
     sig = jax.nn.sigmoid(gate)
     gate_grad = hidden_grad * up * sig * (1.0 + gate * (1.0 - sig))
     up_grad = hidden_grad * (gate * sig)
     gu[:, block_of(u_own, 2 * units)] = jnp.concatenate([gate_grad, up_grad], axis=1).astype(BF16)
-    sent += gather_start(gu, 2 * units, AG)
-    new, on = gather_relay(hf, units, AH)
-    gather_end(hf, units, AH, on)
-    sent += new
-    so[...] = dot(hf[...], wd[...], ((1,), (0,))).reshape(experts, cap, width).astype(BF16)
-    exchange(so, ro, 2)
-    eg[...] = dot(hf[...], gm[...], ((0,), (0,))).astype(BF16)
+    gather_first(sent, gu, 2 * units, AG)
+    gather_on(sent, hf, units, AH, on_first)
+    gather_second(sent, gu, 2 * units, AG)
+    gather_on(sent, hf, units, AH, on_second)
+    gather_on(sent, gu, 2 * units, AG, on_first)
+    gather_on(sent, hf, units, AH, on_last)
+    gather_end(hf, units, AH)
+    row_out = dot(hf[...], wd[...], ((1,), (1,)))
+    so[...] = row_out[:, :body].reshape(experts, cap, body).astype(BF16)
+    sx[:, :, width:] = row_out[:, body:].reshape(experts, cap, rest).astype(BF16)
+    eg[...] = dot(gm[...], hf[...], ((0,), (0,))).astype(BF16)
     trade = remote(eg, er, 50, {"expert": lax.rem(me + experts // 2, experts)})
     trade.start()
-    new, on = gather_relay(gu, 2 * units, AG)
-    gather_end(gu, 2 * units, AG, on)
-    sent += new
-    sx[...] = dot(gu[...], wp[...], ((1,), (1,))).reshape(experts, cap, width).astype(BF16)
+    gather_on(sent, gu, 2 * units, AG, on_second)
+    exchange(so, ro, 2)
+    gather_on(sent, gu, 2 * units, AG, on_last)
+    gather_end(gu, 2 * units, AG)
+    sx[:, :, :width] = dot(gu[...], wp[...], ((1,), (1,))).reshape(experts, cap, width).astype(BF16)
     exchange(sx, rx, 3)
     trade.wait_recv()
     moved = jnp.where(swapped_ref[...] == lax.rem(me, experts // 2), 1.0, 0.0)
@@ -259,15 +278,19 @@
     ed[...] = jnp.where(moved > 0.5, er[...].astype(F32), eg[...].astype(F32)).astype(BF16)
     store = pltpu.make_async_copy(ed, dg_hbm.at[0], lsem.at[0])
     store.start()
+
+    def combined(both):
+        first, second = both[:, :tokens], both[:, tokens:]
+        return rw_ref[0:1, :] * first + rw_ref[1:2, :] * second
+
     arrived(ro, 2)
-    back = ro[...].astype(F32).reshape(rows, width).astype(BF16)
-    total = rw_ref[:, 0:1] * dot(pt[pl.ds(0, tokens), :], back, ((1,), (0,)))
-    total = total + rw_ref[:, 1:2] * dot(pt[pl.ds(tokens, tokens), :], back, ((1,), (0,)))
-    out_ref[...] = total.astype(BF16)
+    back = ro[...].astype(F32).reshape(rows, body).astype(BF16)
+    out_ref[pl.ds(0, body), :] = combined(dot(back, sel[...], ((0,), (0,)))).astype(BF16)
     arrived(rx, 3)
-    both = pt[pl.ds(0, tokens), :] + pt[pl.ds(tokens, tokens), :]
-    back = rx[...].astype(F32).reshape(rows, width).astype(BF16)
-    dx_ref[...] = dot(both, back, ((1,), (0,))).astype(BF16)
+    back = rx[...].astype(F32).reshape(rows, full).astype(BF16)
+    both = dot(back, sel[...], ((0,), (0,)))
+    out_ref[pl.ds(body, rest), :] = combined(both[width:]).astype(BF16)
+    dx_ref[...] = (both[:width, :tokens] + both[:width, tokens:]).astype(BF16)
     for copy in sent:
         copy.wait_send()
     trade.wait_send()
@@ -286,36 +309,44 @@
     rows = experts * cap
     units = hidden // 8
     half = rows // 2
+    body = width // 128 * 128
+    full = 2 * width - body
     vm = lambda *shape: pltpu.VMEM(shape, BF16)
     scratch = [
-        vm(width, 2 * hidden), vm(hidden, width),
-        *[vm(experts, cap, width) for _ in range(8)],
-        vm(rows, width), vm(rows, width), vm(2 * count, rows),
+        vm(width, count), vm(width, count), pltpu.VMEM((routes.shape[1], count), jnp.int32),
+        pltpu.VMEM((routes.shape[1], count), F32), pltpu.VMEM((1, swapped.shape[0]), jnp.int32),
+        vm(width, 2 * hidden), vm(width, hidden), vm(2 * width, 2 * count),
+        *[vm(experts, cap, w) for w in (full, body, full, body, body, full, body, full)],
+        vm(rows, width), vm(rows, width), vm(rows, 2 * count),
         vm(4, 2, rows, 2 * units), vm(4, rows, 2 * units), vm(4, rows, 2 * units),
         vm(2, half, 2 * units), vm(2, half, 2 * units), vm(2, rows, 2 * units),
         pltpu.VMEM((rows, 2 * units), F32),
         vm(4, 2, rows, units), vm(4, rows, units), vm(4, rows, units),
         vm(2, half, units), vm(2, half, units), vm(2, rows, units),
         vm(rows, hidden), vm(rows, 2 * hidden),
-        vm(hidden, width), vm(hidden, width), vm(hidden, width),
+        vm(width, hidden), vm(width, hidden), vm(width, hidden),
         pltpu.SemaphoreType.DMA((SEMS,)), pltpu.SemaphoreType.DMA((SEMS,)),
-        pltpu.SemaphoreType.DMA((17,)),
+        pltpu.SemaphoreType.DMA((22,)),
     ]
     whole = pl.BlockSpec(memory_space=pltpu.VMEM)
     place = pl.BlockSpec(memory_space=pl.ANY)
-    return pl.pallas_call(
+    layer_out, token_grad, down_grad = pl.pallas_call(
         functools.partial(kernel, experts, cap),
         out_shape=(
-            jax.ShapeDtypeStruct((count, width), BF16),
-            jax.ShapeDtypeStruct((count, width), BF16),
-            jax.ShapeDtypeStruct(down_weight.shape, BF16),
+            pltpu.VMEM((width, count), BF16),
+            pltpu.VMEM((width, count), BF16),
+            pltpu.VMEM((1, width, hidden), BF16),
         ),
-        in_specs=[whole, whole, place, place, whole, whole, whole],
+        in_specs=[place] * 7,
         out_specs=(whole, whole, place),
         scratch_shapes=scratch,
-        compiler_params=pltpu.CompilerParams(collective_id=0, has_side_effects=True),
+        compiler_params=pltpu.CompilerParams(collective_id=0, has_side_effects=True, vmem_limit_bytes=58 * 1024 * 1024),
         name="layer",
-    )(tokens, out_grad, gate_up_weight, down_weight, routes, route_weight, swapped.reshape(1, -1))
+    )(
+        tokens.T, out_grad.T, gate_up_weight, down_weight.transpose(0, 2, 1), routes.T,
+        route_weight.T, swapped.reshape(1, -1),
+    )
+    return layer_out.T, token_grad.T, down_grad.transpose(0, 2, 1)
 
 
 def solution(mesh):

time: 193 us -> 177 us (0.917)
  the two profiles are of different devices: /device:TPU:1 before, /device:TPU:121 now
where the time goes in v2:
time: 177 us
  Pallas kernels  174 us (98%)
  local copies, waits for them, and re-layouts  2.22 us (1%)
    pallas_call x1, Pallas kernels, on_device(): pl.pallas_call(functools.partial(kernel, experts, cap), out_shape=(pltpu....  174 us

profile of v2, /device:TPU:121, one launch (start us, length us, event | category | flops | bytes accessed | tf_op | source)
XLA Modules:
  0.0 177.1 jit_solution(1533108516678658924)
XLA Ops:
  0.6 174.3 %layer.1 = (bf16[448,128]{1,0:T(8,128)(2,1)S(1)}, bf16[448,128]{1,0:T(8,128)(2,1)S(1)}, bf16[1,448,1024]{2,1,0:T(8,128)(2,1)S(1)}) custom-call(bf16[448,128]{1,0:T(8,128)(2,1)} %bitcast.13, bf16[448,128]{1,0:T(8,128)(2,1)} %bitcast.14, bf16[1,448,2048]{2,1,0:T(8,128)(2,1)} %wg_hbm.1, bf16[1,448,1024]{2,1,0:T(8,128)(2,1)} %bitcast.12, s32[2,128]{1,0:T(2,128)} %bitcast.15, ...), custom_call_target="tpu_custom_call" | custom-call | tf_op jit(solution)/shard_map/layer/pallas_call | solution.py:333
  174.9 0.6 copy.13
  175.6 0.6 copy.14
  176.2 0.9 copy.15

commit v3 on v2

--- a/solution.py
+++ b/solution.py
@@ -25,7 +25,7 @@
     wp, wd, xt, st, sg, rt, rg, so, sx, ro, rx, tm, gm, sel,
     pg, xg, sgu, relg, augg, fromg, own,
     ph, xh, sh, relh, augh, fromh,
-    hf, gu, eg, er, ed,
+    hf, gu, eg, er, ed, acc,
     ss, rs, lsem,
 ):
     dp = lax.axis_index("dp")
@@ -211,14 +211,33 @@
     on_second = ((low, u_minus, 2, plus, None, 9), (top, u_plus, 3, minus, None, 10))
     on_last = ((top, u_far, 4, plus, None, 11), (low, u_far, 5, minus, None, 12))
 
-    def gather_end(buf, w, base):
-        shift = 1 - 2 * c
-        for rows_of, u, i in (
-            (slice(None), u_own, 6), (top, u_minus, 7), (low, u_plus, 8), (low, u_minus, 9),
-            (top, u_plus, 10), (top, u_far, 11), (low, u_far, 12),
-        ):
-            ref = buf.at[rows_of, block_of(u + shift, w)]
+    over_own = ((slice(None), u_own, 6),)
+    over_near = ((top, u_minus, 7), (low, u_minus, 9), (low, u_plus, 8), (top, u_plus, 10))
+    over_far = ((top, u_far, 11), (low, u_far, 12))
+
+    def gather_over(buf, w, base, steps):
+        for rows_of, u, i in steps:
+            ref = buf.at[rows_of, block_of(u + 1 - 2 * c, w)]
             remote(ref, ref, base + i, other).wait_recv()
+
+    def chip(d, w):
+        return block_of(lax.rem(h + d, 4), w)
+
+    trades = []
+
+    def trade(d):
+        cols = chip(d, 2 * units)
+        eg[:, cols] = dot(gm[...], hf[:, cols], ((0,), (0,))).astype(BF16)
+        copy = remote(
+            eg.at[:, cols], er.at[:, cols], 50 + d,
+            {"expert": lax.rem(me + experts // 2, experts)},
+        )
+        copy.start()
+        trades.append(copy)
+
+    def dx_part(d):
+        cols = chip(d, 4 * units)
+        return dot(gu[:, cols], wp[:, cols], ((1,), (1,)))
 
     sent = []
     arrived(rt, 0)
@@ -247,6 +266,8 @@
     hf[:, block_of(u_own, units)] = (gate * jax.nn.sigmoid(gate) * up).astype(BF16)
     gather_first(sent, hf, units, AH)
     gather_second(sent, hf, units, AH)
+    gather_over(hf, units, AH, over_own)
+    trade(0)
     hidden_grad = reduce_end(sh, fromh, RH)
     gate, up = own[:, :units], own[:, units:]
     sig = jax.nn.sigmoid(gate)
@@ -257,22 +278,28 @@
     gather_on(sent, hf, units, AH, on_first)
     gather_second(sent, gu, 2 * units, AG)
     gather_on(sent, hf, units, AH, on_second)
+    gather_over(hf, units, AH, over_near)
+    trade(1)
+    trade(3)
+    gather_over(gu, 2 * units, AG, over_own)
+    acc[...] = dx_part(0)
     gather_on(sent, gu, 2 * units, AG, on_first)
     gather_on(sent, hf, units, AH, on_last)
-    gather_end(hf, units, AH)
+    gather_over(hf, units, AH, over_far)
+    trade(2)
     row_out = dot(hf[...], wd[...], ((1,), (1,)))
     so[...] = row_out[:, :body].reshape(experts, cap, body).astype(BF16)
     sx[:, :, width:] = row_out[:, body:].reshape(experts, cap, rest).astype(BF16)
-    eg[...] = dot(gm[...], hf[...], ((0,), (0,))).astype(BF16)
-    trade = remote(eg, er, 50, {"expert": lax.rem(me + experts // 2, experts)})
-    trade.start()
     gather_on(sent, gu, 2 * units, AG, on_second)
     exchange(so, ro, 2)
+    gather_over(gu, 2 * units, AG, over_near)
+    acc[...] = acc[...] + dx_part(1) + dx_part(3)
     gather_on(sent, gu, 2 * units, AG, on_last)
-    gather_end(gu, 2 * units, AG)
-    sx[:, :, :width] = dot(gu[...], wp[...], ((1,), (1,))).reshape(experts, cap, width).astype(BF16)
+    gather_over(gu, 2 * units, AG, over_far)
+    sx[:, :, :width] = (acc[...] + dx_part(2)).reshape(experts, cap, width).astype(BF16)
     exchange(sx, rx, 3)
-    trade.wait_recv()
+    for copy in trades:
+        copy.wait_recv()
     moved = jnp.where(swapped_ref[...] == lax.rem(me, experts // 2), 1.0, 0.0)
     moved = jnp.max(moved, axis=1, keepdims=True)
     ed[...] = jnp.where(moved > 0.5, er[...].astype(F32), eg[...].astype(F32)).astype(BF16)
@@ -293,7 +320,8 @@
     dx_ref[...] = (both[:width, :tokens] + both[:width, tokens:]).astype(BF16)
     for copy in sent:
         copy.wait_send()
-    trade.wait_send()
+    for copy in trades:
+        copy.wait_send()
     departed(st, 0)
     departed(sg, 1)
     departed(so, 2)
@@ -325,6 +353,7 @@
         vm(2, half, units), vm(2, half, units), vm(2, rows, units),
         vm(rows, hidden), vm(rows, 2 * hidden),
         vm(width, hidden), vm(width, hidden), vm(width, hidden),
+        pltpu.VMEM((rows, width), F32),
         pltpu.SemaphoreType.DMA((SEMS,)), pltpu.SemaphoreType.DMA((SEMS,)),
         pltpu.SemaphoreType.DMA((22,)),
     ]

time: 177 us -> 170 us (0.960)
  the two profiles are of different devices: /device:TPU:121 before, /device:TPU:1 now
where the time goes in v3:
time: 170 us
  Pallas kernels  167 us (98%)
  local copies, waits for them, and re-layouts  2.22 us (1%)
    pallas_call x1, Pallas kernels, on_device(): pl.pallas_call(functools.partial(kernel, experts, cap), out_shape=(pltpu....  167 us

profile of v3, /device:TPU:1, one launch (start us, length us, event | category | flops | bytes accessed | tf_op | source)
XLA Modules:
  0.0 169.8 jit_solution(5987336216956367710)
XLA Ops:
  0.6 167.0 %layer.1 = (bf16[448,128]{1,0:T(8,128)(2,1)S(1)}, bf16[448,128]{1,0:T(8,128)(2,1)S(1)}, bf16[1,448,1024]{2,1,0:T(8,128)(2,1)S(1)}) custom-call(bf16[448,128]{1,0:T(8,128)(2,1)} %bitcast.13, bf16[448,128]{1,0:T(8,128)(2,1)} %bitcast.14, bf16[1,448,2048]{2,1,0:T(8,128)(2,1)} %wg_hbm.1, bf16[1,448,1024]{2,1,0:T(8,128)(2,1)} %bitcast.12, s32[2,128]{1,0:T(2,128)} %bitcast.15, ...), custom_call_target="tpu_custom_call" | custom-call | tf_op jit(solution)/shard_map/layer/pallas_call | solution.py:362
  167.6 0.6 copy.13
  168.3 0.6 copy.14
  168.9 0.9 copy.15
